TPU v7x, 128 devices: a whole 4x4x4 slice. The times are simulated.
128 devices in a mesh: rep: 32 (over y, z, core), feat: 4 (over x).
Axes of the slice: x: 4, y: 4, z: 4, core: 2. Of those that a mesh axis runs over, the one named last changes fastest.
Arguments:
- activations: bfloat16 [32768, 8192], P('rep', 'feat'), may hold values from -6 to 6
- out_grad: bfloat16 [32768, 512], P(('rep', 'feat')), may hold values from -6 to 6
- weight: float32 [8192, 512], P('feat'), may hold values from -0.25 to 0.25
- momentum: float32 [32, 8192, 512], P('rep', 'feat'), may hold values from -4 to 4
- select: int32 [32, 32], replicated, may hold values from 0 to 4095, as said below
Outputs:
- input_grad: float32 [32768, 8192], P('rep', 'feat')
- residual: float32 [32, 8192, 512], P('rep', 'feat')
- new_weight: float32 [8192, 512], P('feat')
Inputs may be any that keep to these rules, and one draw needn't show every extreme that they name: `select`: each replica's row holds 32 distinct frequency rows.
All inputs are finite; a program needn't handle non-finite values.
Results may differ from a plain program's by a relative error of at most 0.0003.
Values may be sent and summed in bfloat16 or wider, within the bound.
A program may use at most 128 MiB of HBM per device.

v0:
```python
import functools

import jax
import jax.numpy as jnp
from jax import lax
from jax.experimental import pallas as pl
from jax.experimental.pallas import tpu as pltpu
from jax.sharding import PartitionSpec as P

CH = 64
MOMENTUM_DECAY = 0.9
STEP_RATE = 0.5
f32 = jnp.float32
bf16 = jnp.bfloat16
NN = (((1,), (0,)), ((), ()))
NT = (((1,), (1,)), ((), ()))
TN = (((0,), (0,)), ((), ()))
MIB = 1 << 20


def dot(a, b, dims, precision=None):
    return lax.dot_general(a, b, dims, precision=precision, preferred_element_type=f32)


def split(v):
    high = v.astype(bf16)
    return high, (v - high.astype(f32)).astype(bf16)


def dct_transposed():
    a = lax.broadcasted_iota(jnp.int32, (CH, CH), 0)
    u = lax.broadcasted_iota(jnp.int32, (CH, CH), 1)
    turn = ((2 * a + 1) * u) & 255
    table = jnp.cos(turn.astype(f32) * f32(jnp.pi / 128)) * f32((2.0 / CH) ** 0.5)
    return jnp.where(u == 0, f32((1.0 / CH) ** 0.5), table)


def pick(table, row):
    n = row.shape[1]
    hot = (lax.broadcasted_iota(jnp.int32, (CH, n), 0) == jnp.broadcast_to(row, (CH, n))).astype(f32)
    return dot(table, hot, NN, lax.Precision.HIGHEST)


def rep_of(c, q, p):
    return (1 - c) * (q * 8 + p * 2) + c * (p * 8 + q * 2 + 1)


def first_kernel(
    x_hbm, g_hbm, w_hbm, mom_hbm, sel_ref,
    m_ref, grad_ref, eh_ref, el_ref, call_ref, wv,
    xv, gv, but, bvt, bve, bu4, cown,
    local_sem, g_send, g_recv, c_send, c_recv,
):
    feat = lax.axis_index("feat")
    rep = lax.axis_index("rep")
    c = rep % 2
    z = (rep // 2) % 4
    y = rep // 8
    p = (1 - c) * z + c * y
    q = (1 - c) * y + c * z
    slot = c * 16 + q * 4 + p
    right, left, across = (feat + 1) % 4, (feat + 3) % 4, (feat + 2) % 4
    near = [rep_of(c, q, (p + s) % 4) for s in (1, 2, 3)]
    far = [rep_of(c, (q + s) % 4, p) for s in (1, 2, 3)]
    partner = rep + 1 - 2 * c

    blocks = (feat, left, right, across)
    own_g = pltpu.make_async_copy(g_hbm, gv.at[pl.ds(feat * 256, 256)], local_sem.at[0])
    own_g.start()
    x_copies = []
    for n, b in enumerate(blocks):
        rows = pl.ds(b * 256, 256)
        x_copies.append(pltpu.make_async_copy(x_hbm.at[rows], xv.at[rows], local_sem.at[1 + n]))
    w_copies = [
        pltpu.make_async_copy(w_hbm.at[:, pl.ds(n * 128, 128)], wv.at[n], local_sem.at[7 + n]) for n in range(4)
    ]
    m_copy = pltpu.make_async_copy(mom_hbm, m_ref, local_sem.at[5])
    x_copies[0].start()
    for cp in w_copies:
        cp.start()
    m_copy.start()
    for cp in x_copies[1:]:
        cp.start()

    barrier = pltpu.get_barrier_semaphore()
    for f in (left, right):
        pl.semaphore_signal(barrier, inc=1, device_id={"feat": f})
    for r in near + far + [partner]:
        pl.semaphore_signal(barrier, inc=1, device_id={"rep": r})
    pl.semaphore_wait(barrier, 9)

    def g_copy(n, block, half, to, src=None):
        rows = pl.ds(block * 256 + half * 128, 128)
        return pltpu.make_async_remote_copy(
            src_ref=gv.at[rows] if src is None else src,
            dst_ref=gv.at[rows],
            send_sem=g_send.at[n],
            recv_sem=g_recv.at[n],
            device_id={"feat": to},
        )

    sends = [
        g_copy(0, feat, 0, right, g_hbm.at[pl.ds(0, 128)]),
        g_copy(1, feat, 1, left, g_hbm.at[pl.ds(128, 128)]),
        g_copy(2, feat, 1, right, g_hbm.at[pl.ds(128, 128)]),
        g_copy(3, feat, 0, left, g_hbm.at[pl.ds(0, 128)]),
    ]
    for cp in sends:
        cp.start()
    arrive = [
        g_copy(0, left, 0, right),
        g_copy(1, right, 1, left),
        g_copy(2, left, 1, right),
        g_copy(3, right, 0, left),
        g_copy(4, across, 0, right),
        g_copy(5, across, 1, left),
    ]

    table = dct_transposed()
    sel = sel_ref[...]
    rows = []
    for s in range(32):
        r = rep_of(s // 16, (s % 16) // 4, s % 4)
        rows.append(sel[r : r + 1, :])
    flat = jnp.concatenate(rows, axis=1)
    but[...] = pick(table, flat >> 6)
    bvt[...] = pick(table, flat & 63)
    mine = sel_ref[pl.ds(rep, 1), :]
    mine = jnp.concatenate([mine] * 4, axis=1)
    bu4[...] = pick(table, mine >> 6)
    bv4 = pick(table, mine & 63)
    tall = jnp.concatenate([bv4] * 4, axis=0)
    ahead = lax.broadcasted_iota(jnp.int32, (256, 128), 0) // 64
    along = lax.broadcasted_iota(jnp.int32, (256, 128), 1) // 32
    bve[...] = jnp.where(ahead == along, tall, f32(0))

    def outer(a):
        high, low = split(but[pl.ds(a, 1), :] * bvt[...])
        at = pl.ds(pl.multiple_of(a * CH, CH), CH)
        eh_ref[at, :] = high
        el_ref[at, :] = low

    @pl.loop(0, 24)
    def _(a):
        outer(a)

    arrive[0].wait_recv()
    forward_right = g_copy(4, left, 0, right)
    forward_right.start()
    arrive[1].wait_recv()
    forward_left = g_copy(5, right, 1, left)
    forward_left.start()

    @pl.loop(24, 64)
    def _(a):
        outer(a)

    def weight_grad(block, first):
        rows = pl.ds(pl.multiple_of(block * 256, 256), 256)

        @pl.loop(0, 8)
        def _(n):
            at = pl.ds(pl.multiple_of(n * 256, 256), 256)
            part = dot(xv[rows, at], gv[rows, :], TN) * f32(1.0 / 1024)
            if first:
                m_ref[at, :] = f32(MOMENTUM_DECAY) * m_ref[at, :] + part
            else:
                m_ref[at, :] = m_ref[at, :] + part

    def input_grad(block, n0, n1):
        rows = pl.ds(pl.multiple_of(block * 256, 256), 256)

        @pl.loop(n0, n1)
        def _(step):
            at = pl.ds(pl.multiple_of(step * 256, 256), 256)
            high, low = split(jnp.concatenate([wv[n, at, :] for n in range(4)], axis=1))
            gb = gv[rows, :]
            grad_ref[rows, at] = dot(gb, high, NT) + dot(gb, low, NT)

    own_g.wait()
    x_copies[0].wait()
    m_copy.wait()
    weight_grad(feat, True)
    for cp in w_copies:
        cp.wait()
    input_grad(feat, 0, 8)
    arrive[2].wait_recv()
    x_copies[1].wait()
    weight_grad(left, False)
    arrive[3].wait_recv()
    x_copies[2].wait()
    weight_grad(right, False)
    input_grad(left, 0, 8)
    input_grad(right, 0, 8)
    arrive[4].wait_recv()
    arrive[5].wait_recv()
    x_copies[3].wait()
    weight_grad(across, False)

    @pl.loop(0, 4)
    def _(n):
        at = pl.ds(pl.multiple_of(n * 512, 512), 512)
        to = pl.ds(pl.multiple_of(n * 8, 8), 8)
        for h in range(2):
            inner = dot(m_ref[at, h * 256 : h * 256 + 256], bve[...], NN, lax.Precision.HIGH)
            cown[to, h * 128 : h * 128 + 128] = jnp.sum(inner.reshape(8, CH, 128) * bu4[...][None], axis=1)

    turned = cown[...].T
    call_ref[slot] = jnp.concatenate([turned[j * 32 : j * 32 + 32, :] for j in range(8)], axis=1)

    def c_copy(n, at, to):
        return pltpu.make_async_remote_copy(
            src_ref=call_ref.at[at],
            dst_ref=call_ref.at[at],
            send_sem=c_send.at[n],
            recv_sem=c_recv.at[at],
            device_id={"rep": to},
        )

    out = []

    def send(at, to):
        cp = c_copy(len(out), at, to)
        cp.start()
        out.append(cp)

    for r in near + far + [partner]:
        send(slot, r)

    def take_away(n0, n1):
        @pl.loop(n0, n1)
        def _(n):
            at = pl.ds(pl.multiple_of(n * 512, 512), 512)
            to = pl.ds(pl.multiple_of(n * 8, 8), 8)
            for h in range(2):
                cols = slice(h * 256, h * 256 + 256)
                field = cown[to, h * 128 : h * 128 + 128][:, None, :] * bu4[...][None]
                back = dot(field.reshape(512, 128), bve[...], NT, lax.Precision.HIGH)
                m_ref[at, cols] = m_ref[at, cols] - back

    input_grad(across, 0, 4)
    for s in (1, 3, 2):
        at = c * 16 + q * 4 + (p + s) % 4
        c_copy(0, at, partner).wait_recv()
        for r in far + [partner]:
            send(at, r)
    input_grad(across, 4, 8)
    take_away(0, 4)
    for t in range(4):
        for s in (1, 3, 2):
            at = c * 16 + ((q + s) % 4) * 4 + (p + t) % 4
            c_copy(0, at, partner).wait_recv()
            send(at, partner)
    for n in range(16):
        c_copy(0, (1 - c) * 16 + n, partner).wait_recv()
    for cp in sends + [forward_right, forward_left] + out:
        cp.wait_send()


def second_kernel(
    m_ref, grad_ref, eh_ref, el_ref, call_ref, w_ref, grad_hbm, res_hbm, new_hbm, nw, lh, ll, sems
):
    copies = [
        pltpu.make_async_copy(m_ref, res_hbm, sems.at[0]),
        pltpu.make_async_copy(grad_ref, grad_hbm, sems.at[1]),
    ]
    for cp in copies:
        cp.start()
    high, low = split(call_ref[...].reshape(1024, 256).T)
    lh[...] = high
    ll[...] = low
    low_half = lax.broadcasted_iota(jnp.int32, (32, 128), 1) < 64

    @pl.loop(0, 16)
    def _(n):
        at = pl.ds(pl.multiple_of(n * 256, 256), 256)
        eh = eh_ref[at, :]
        total = dot(lh[...], eh, NT) + dot(ll[...], eh, NT) + dot(lh[...], el_ref[at, :], NT)
        total = total * f32(STEP_RATE)
        for h in range(2):
            for j in range(4):
                one = total[j * 64 : j * 64 + 32, h * 128 : h * 128 + 128]
                two = total[j * 64 + 32 : j * 64 + 64, h * 128 : h * 128 + 128]
                even = jnp.where(low_half, one, pltpu.roll(two, 64, 1))
                odd = jnp.where(low_half, pltpu.roll(one, 64, 1), two)
                for k, v in enumerate((even, odd)):
                    rows = pl.ds(n * 4 + h * 2 + k, 32, stride=CH)
                    nw[j, rows, :] = w_ref[j, rows, :] - v

    for n in range(4):
        cp = pltpu.make_async_copy(nw.at[n], new_hbm.at[:, pl.ds(n * 128, 128)], sems.at[2 + n])
        cp.start()
        copies.append(cp)
    for cp in copies:
        cp.wait()


def vmem(shape, dtype):
    return pltpu.VMEM(shape, dtype)


def body(x, g, w, mom, sel):
    any_space = pl.BlockSpec(memory_space=pl.ANY)
    vm = pl.BlockSpec(memory_space=pltpu.VMEM)
    mid = pl.pallas_call(
        first_kernel,
        out_shape=(
            vmem((2048, 512), f32),
            vmem((1024, 2048), f32),
            vmem((4096, 1024), bf16),
            vmem((4096, 1024), bf16),
            vmem((32, 32, 256), f32),
            vmem((4, 2048, 128), f32),
        ),
        in_specs=[any_space] * 4 + [vm],
        out_specs=[vm] * 6,
        scratch_shapes=[
            pltpu.VMEM((1024, 2048), bf16),
            pltpu.VMEM((1024, 512), bf16),
            pltpu.VMEM((CH, 1024), f32),
            pltpu.VMEM((CH, 1024), f32),
            pltpu.VMEM((256, 128), f32),
            pltpu.VMEM((CH, 128), f32),
            pltpu.VMEM((32, 256), f32),
            pltpu.SemaphoreType.DMA((11,)),
            pltpu.SemaphoreType.DMA((6,)),
            pltpu.SemaphoreType.DMA((6,)),
            pltpu.SemaphoreType.DMA((31,)),
            pltpu.SemaphoreType.DMA((32,)),
        ],
        compiler_params=pltpu.CompilerParams(
            collective_id=0, has_side_effects=True, vmem_limit_bytes=12 * MIB
        ),
        name="gather_and_select",
    )(*(pltpu.with_memory_space_constraint(v, pltpu.HBM) for v in (x, g, w, mom[0])), sel)
    grad, res, new = pl.pallas_call(
        second_kernel,
        out_shape=(
            jax.ShapeDtypeStruct((1024, 2048), f32),
            jax.ShapeDtypeStruct((2048, 512), f32),
            jax.ShapeDtypeStruct((2048, 512), f32),
        ),
        in_specs=[vm] * 6,
        out_specs=[any_space] * 3,
        scratch_shapes=[
            pltpu.VMEM((4, 2048, 128), f32),
            pltpu.VMEM((256, 1024), bf16),
            pltpu.VMEM((256, 1024), bf16),
            pltpu.SemaphoreType.DMA((6,)),
        ],
        compiler_params=pltpu.CompilerParams(vmem_limit_bytes=12 * MIB),
        name="decode_and_write",
    )(*(pltpu.with_memory_space_constraint(v, pltpu.VMEM) for v in mid))
    return grad, res[None], new


def solution(mesh):
    in_specs = (P("rep", "feat"), P(("rep", "feat"), None), P("feat", None), P("rep", "feat", None), P())
    out_specs = (P("rep", "feat"), P("rep", "feat", None), P("feat", None))
    return jax.shard_map(body, mesh=mesh, in_specs=in_specs, out_specs=out_specs, check_vma=False)
```

profile of v0, /device:TPU:1, one launch (start us, length us, event | category | flops | bytes accessed | tf_op | source)
XLA Modules:
  0.0 64.9 jit_solution(11132960186651847934)
XLA Ops:
  0.6 0.0 copy-start
  0.6 0.7 %copy-done = s32[32,32]{1,0:T(8,128)S(1)} copy-done((s32[32,32]{1,0:T(8,128)S(1)}, s32[32,32]{1,0:T(8,128)}, u32[]{:S(2)}) %copy-start) | copy-done | bytes 4120
  1.4 46.5 %gather_and_select.1 = (f32[2048,512]{1,0:T(8,128)S(1)}, f32[1024,2048]{1,0:T(8,128)S(1)}, bf16[4096,1024]{1,0:T(8,128)(2,1)S(1)}, bf16[4096,1024]{1,0:T(8,128)(...) custom-call(bf16[1024,2048]{1,0:T(8,128)(2,1)} %x_hbm.1, bf16[256,512]{1,0:T(8,128)(2,1)} %g_hbm.1, ...), custom_call_target="tpu_custom_call" | custom-call | tf_op jit(solution)/shard_map/gather_and_select/pallas_call | solution.py:305
  47.8 17.1 %decode_and_write.1 = (f32[1024,2048]{1,0:T(8,128)}, f32[2048,512]{1,0:T(8,128)}, f32[2048,512]{1,0:T(8,128)}) custom-call(f32[2048,512]{1,0:T(8,128)S(1)} %get-tuple-element.12.m_ref, f32[1024,2048]{1,0:T(8,128)S(1)} %get-tuple-element.13.grad_ref, bf16[4096,1024]{1,0:T(8,128)(2,1)S(1)} %get-tuple-element.14.eh_ref, ...), custom_call_target="tpu_custom_call" | custom-call | tf_op jit(solution)/shard_map/decode_and_write/pallas_call | solution.py:336
Async XLA Ops:
  0.6 0.7 %copy-start = (s32[32,32]{1,0:T(8,128)S(1)}, s32[32,32]{1,0:T(8,128)}, u32[]{:S(2)}) copy-start(s32[32,32]{1,0:T(8,128)} %sel_ref.1) | copy-start | bytes 12292
where the time goes:
time: 65.1 us; the launch traced here: 64.9 us
  Pallas kernels  63.5 us (98%)
  local copies, waits for them, and re-layouts  0.71 us (1%)
    pallas_call x1, Pallas kernels, body(): pl.pallas_call(first_kernel, out_shape=(vmem((2048, 512), f32), vmem((102...  46.5 us
    pallas_call x1, Pallas kernels, body(): pl.pallas_call(second_kernel, out_shape=(jax.ShapeDtypeStruct((1024, 2048...  17.1 us

commit v1 on v0

v1 whole, which is shorter than its diff:
```python
import functools

import jax
import jax.numpy as jnp
from jax import lax
from jax.experimental import pallas as pl
from jax.experimental.pallas import tpu as pltpu
from jax.sharding import PartitionSpec as P

CH = 64
MOMENTUM_DECAY = 0.9
STEP_RATE = 0.5
f32 = jnp.float32
bf16 = jnp.bfloat16
NN = (((1,), (0,)), ((), ()))
NT = (((1,), (1,)), ((), ()))
TN = (((0,), (0,)), ((), ()))
MIB = 1 << 20


def dot(a, b, dims, precision=None):
    return lax.dot_general(a, b, dims, precision=precision, preferred_element_type=f32)


def split(v):
    high = v.astype(bf16)
    return high, (v - high.astype(f32)).astype(bf16)


def dct_transposed():
    a = lax.broadcasted_iota(jnp.int32, (CH, CH), 0)
    u = lax.broadcasted_iota(jnp.int32, (CH, CH), 1)
    turn = ((2 * a + 1) * u) & 255
    table = jnp.cos(turn.astype(f32) * f32(jnp.pi / 128)) * f32((2.0 / CH) ** 0.5)
    return jnp.where(u == 0, f32((1.0 / CH) ** 0.5), table)


def pick(table, row):
    n = row.shape[1]
    hot = (lax.broadcasted_iota(jnp.int32, (CH, n), 0) == jnp.broadcast_to(row, (CH, n))).astype(f32)
    return dot(table, hot, NN, lax.Precision.HIGHEST)


def offsets():
    both = [(dy, dz) for dy in range(4) for dz in range(4) if (dy, dz) != (0, 0)]
    return sorted(both, key=lambda o: (min(o[0], 4 - o[0]) + min(o[1], 4 - o[1]), o))


def first_kernel(
    x_hbm, g_hbm, w_hbm, mom_hbm, sel_ref,
    m_ref, grad_ref, eh_ref, el_ref, oth_ref, acc_ref, wv,
    xv, xt, gv, but, bvt, bhl, bhh, bu4, cown, own_ref,
    local_sem, g_send, g_recv, c_send, own_recv, oth_recv,
):
    feat = lax.axis_index("feat")
    rep = lax.axis_index("rep")
    core = rep % 2
    chip = rep // 2
    y, z = chip // 4, chip % 4
    partner = rep + 1 - 2 * core
    right, left, across = (feat + 1) % 4, (feat + 3) % 4, (feat + 2) % 4
    blocks = (feat, left, right, across)

    def chip_at(dy, dz):
        return (y + dy) % 4 * 4 + (z + dz) % 4

    own_g = pltpu.make_async_copy(g_hbm, gv.at[pl.ds(0, 256)], local_sem.at[0])
    own_g.start()
    x_copies = [
        pltpu.make_async_copy(x_hbm.at[pl.ds(b * 256, 256)], xv.at[pl.ds(n * 256, 256)], local_sem.at[1 + n])
        for n, b in enumerate(blocks)
    ]
    m_copy = pltpu.make_async_copy(mom_hbm, m_ref, local_sem.at[5])
    w_copies = [
        pltpu.make_async_copy(w_hbm.at[:, pl.ds(n * 128, 128)], wv.at[n], local_sem.at[6 + n]) for n in range(4)
    ]
    for cp in x_copies + w_copies + [m_copy]:
        cp.start()

    barrier = pltpu.get_barrier_semaphore()
    for f in (left, right):
        pl.semaphore_signal(barrier, inc=1, device_id={"feat": f})
    for dy, dz in offsets():
        pl.semaphore_signal(barrier, inc=1, device_id={"rep": chip_at(dy, dz) * 2 + core})
    pl.semaphore_signal(barrier, inc=1, device_id={"rep": partner})

    table = dct_transposed()
    rows = []
    for s in range(32):
        plane = core if s < 16 else 1 - core
        rows.append(sel_ref[pl.ds((s % 16) * 2 + plane, 1), :])
    flat = jnp.concatenate(rows, axis=1)
    but[...] = pick(table, flat >> 6)
    bvt[...] = pick(table, flat & 63)
    mine = sel_ref[pl.ds(rep, 1), :]
    mine = jnp.concatenate([mine] * 4, axis=1)
    bu4[...] = pick(table, mine >> 6)
    tall = jnp.concatenate([pick(table, mine & 63)] * 4, axis=0)
    ahead = lax.broadcasted_iota(jnp.int32, (256, 128), 0) // 64
    along = lax.broadcasted_iota(jnp.int32, (256, 128), 1) // 32
    high, low = split(jnp.where(ahead == along, tall, f32(0)))
    bhl[:, :128] = high
    bhl[:, 128:] = low
    bhh[:, :128] = high
    bhh[:, 128:] = high

    pl.semaphore_wait(barrier, 18)

    def g_copy(n, slot, half, to, src=None):
        rows = pl.ds(slot * 256 + half * 128, 128)
        return pltpu.make_async_remote_copy(
            src_ref=src,
            dst_ref=gv.at[rows],
            send_sem=g_send.at[n],
            recv_sem=g_recv.at[n],
            device_id={"feat": to},
        )

    halves = [g_hbm.at[pl.ds(0, 128)], g_hbm.at[pl.ds(128, 128)]]
    sends = [
        g_copy(0, 1, 0, right, halves[0]),
        g_copy(1, 2, 1, left, halves[1]),
        g_copy(2, 1, 1, right, halves[1]),
        g_copy(3, 2, 0, left, halves[0]),
    ]
    for cp in sends:
        cp.start()
    sends.append(g_copy(4, 3, 0, right, gv.at[pl.ds(256, 128)]))
    sends.append(g_copy(5, 3, 1, left, gv.at[pl.ds(512 + 128, 128)]))

    def outer(a):
        high, low = split(but[pl.ds(a, 1), :] * bvt[...])
        at = pl.ds(pl.multiple_of(a * CH, CH), CH)
        eh_ref[at, :] = high
        el_ref[at, :] = low

    def turn(slot):
        x_copies[slot].wait()

        @pl.loop(0, 8)
        def _(n):
            at = pl.ds(pl.multiple_of(n * 256, 256), 256)
            xt[slot, at, :] = xv[slot * 256 : slot * 256 + 256, at].T

    turn(0)

    @pl.loop(0, 36)
    def _(a):
        outer(a)

    sends[0].wait_recv()
    sends[4].start()
    sends[1].wait_recv()
    sends[5].start()

    @pl.loop(36, 64)
    def _(a):
        outer(a)

    for slot in (1, 2, 3):
        turn(slot)
    own_g.wait()
    m_copy.wait()
    sends[2].wait_recv()
    sends[3].wait_recv()
    for n in range(4):
        at = slice(n * 512, n * 512 + 512)
        lhs = jnp.concatenate([xt[s, at, :] for s in range(3)], axis=1)
        m_ref[at, :] = f32(MOMENTUM_DECAY) * m_ref[at, :] + dot(lhs, gv[0:768, :], NN) * f32(1.0 / 1024)
    sends[4].wait_recv()
    sends[5].wait_recv()
    for n in range(4):
        at = slice(n * 512, n * 512 + 512)
        m_ref[at, :] = m_ref[at, :] + dot(xt[3, at, :], gv[768:1024, :], NN) * f32(1.0 / 1024)

    for n in range(4):
        for h in range(2):
            high, low = split(m_ref[n * 512 : n * 512 + 512, h * 256 : h * 256 + 256])
            wide = dot(high, bhl[...], NN)
            inner = wide[:, :128] + wide[:, 128:] + dot(low, bhl[:, :128], NN)
            cown[n * 8 : n * 8 + 8, h * 128 : h * 128 + 128] = jnp.sum(
                inner.reshape(8, CH, 128) * bu4[...][None], axis=1
            )
    turned = cown[...].T
    own_ref[chip] = jnp.concatenate([turned[j * 32 : j * 32 + 32, :] for j in range(8)], axis=1)

    gone = []

    def send(dst, sem, at, to):
        cp = pltpu.make_async_remote_copy(
            src_ref=own_ref.at[at],
            dst_ref=dst.at[at],
            send_sem=c_send.at[len(gone)],
            recv_sem=sem.at[at],
            device_id={"rep": to},
        )
        cp.start()
        gone.append(cp)

    def arrived(ref, sem, at):
        pltpu.make_async_remote_copy(
            src_ref=ref.at[at], dst_ref=ref.at[at], send_sem=c_send.at[0], recv_sem=sem.at[at],
            device_id={"rep": partner},
        ).wait_recv()

    for dy, dz in offsets():
        send(own_ref, own_recv, chip, chip_at(dy, dz) * 2 + core)
    send(oth_ref, oth_recv, chip, partner)

    def pass_on(n0, n1):
        for dy, dz in offsets()[n0:n1]:
            at = chip_at(-dy, -dz)
            arrived(own_ref, own_recv, at)
            send(oth_ref, oth_recv, at, partner)

    def take_away(n):
        for h in range(2):
            at, cols = slice(n * 512, n * 512 + 512), slice(h * 256, h * 256 + 256)
            field = cown[n * 8 : n * 8 + 8, h * 128 : h * 128 + 128][:, None, :] * bu4[...][None]
            high, low = split(field.reshape(512, 128))
            back = dot(jnp.concatenate([high, low], axis=1), bhh[...], NT) + dot(high, bhl[:, 128:], NT)
            m_ref[at, cols] = m_ref[at, cols] - back

    def input_grad(n):
        cols = slice(n * 512, n * 512 + 512)
        high, low = split(jnp.concatenate([wv[k, cols, :] for k in range(4)], axis=1))
        part = dot(gv[...], high, NT) + dot(gv[...], low, NT)
        for s, b in enumerate(blocks):
            grad_ref[pl.ds(pl.multiple_of(b * 256, 256), 256), cols] = part[s * 256 : s * 256 + 256, :]

    for n in range(4):
        take_away(n)
    for cp in w_copies:
        cp.wait()
    input_grad(0)
    pass_on(0, 4)
    input_grad(1)
    pass_on(4, 8)
    input_grad(2)
    pass_on(8, 12)
    input_grad(3)
    pass_on(12, 15)

    high, low = split(own_ref[...].reshape(512, 256).T)
    for n in range(8):
        at = slice(n * 512, n * 512 + 512)
        eh = eh_ref[at, 0:512]
        acc_ref[:, at] = dot(high, eh, NT) + dot(low, eh, NT) + dot(high, el_ref[at, 0:512], NT)

    for n in range(16):
        arrived(oth_ref, oth_recv, n)
    for cp in sends + gone:
        cp.wait_send()


def second_kernel(
    m_ref, grad_ref, eh_ref, el_ref, oth_ref, acc_ref, w_ref, grad_hbm, res_hbm, new_hbm, nw, sems
):
    copies = [
        pltpu.make_async_copy(m_ref, res_hbm, sems.at[0]),
        pltpu.make_async_copy(grad_ref, grad_hbm, sems.at[1]),
    ]
    for cp in copies:
        cp.start()
    high, low = split(oth_ref[...].reshape(512, 256).T)
    low_half = lax.broadcasted_iota(jnp.int32, (32, 128), 1) < 64
    for n in range(8):
        at = slice(n * 512, n * 512 + 512)
        eh = eh_ref[at, 512:]
        total = acc_ref[:, at] + dot(high, eh, NT) + dot(low, eh, NT) + dot(high, el_ref[at, 512:], NT)
        total = total * f32(STEP_RATE)
        for h in range(4):
            for j in range(4):
                one = total[j * 64 : j * 64 + 32, h * 128 : h * 128 + 128]
                two = total[j * 64 + 32 : j * 64 + 64, h * 128 : h * 128 + 128]
                even = jnp.where(low_half, one, pltpu.roll(two, 64, 1))
                odd = jnp.where(low_half, pltpu.roll(one, 64, 1), two)
                for k, v in enumerate((even, odd)):
                    rows = pl.ds(n * 8 + h * 2 + k, 32, stride=CH)
                    nw[j, rows, :] = w_ref[j, rows, :] - v
    for n in range(4):
        cp = pltpu.make_async_copy(nw.at[n], new_hbm.at[:, pl.ds(n * 128, 128)], sems.at[2 + n])
        cp.start()
        copies.append(cp)
    for cp in copies:
        cp.wait()


def vmem(shape, dtype):
    return pltpu.VMEM(shape, dtype)


def body(x, g, w, mom, sel):
    any_space = pl.BlockSpec(memory_space=pl.ANY)
    vm = pl.BlockSpec(memory_space=pltpu.VMEM)
    mid = pl.pallas_call(
        first_kernel,
        out_shape=(
            vmem((2048, 512), f32),
            vmem((1024, 2048), f32),
            vmem((4096, 1024), bf16),
            vmem((4096, 1024), bf16),
            vmem((16, 32, 256), f32),
            vmem((256, 4096), f32),
            vmem((4, 2048, 128), f32),
        ),
        in_specs=[any_space] * 4 + [vm],
        out_specs=[vm] * 7,
        scratch_shapes=[
            pltpu.VMEM((1024, 2048), bf16),
            pltpu.VMEM((4, 2048, 256), bf16),
            pltpu.VMEM((1024, 512), bf16),
            pltpu.VMEM((CH, 1024), f32),
            pltpu.VMEM((CH, 1024), f32),
            pltpu.VMEM((256, 256), bf16),
            pltpu.VMEM((256, 256), bf16),
            pltpu.VMEM((CH, 128), f32),
            pltpu.VMEM((32, 256), f32),
            pltpu.VMEM((16, 32, 256), f32),
            pltpu.SemaphoreType.DMA((10,)),
            pltpu.SemaphoreType.DMA((6,)),
            pltpu.SemaphoreType.DMA((6,)),
            pltpu.SemaphoreType.DMA((31,)),
            pltpu.SemaphoreType.DMA((16,)),
            pltpu.SemaphoreType.DMA((16,)),
        ],
        compiler_params=pltpu.CompilerParams(
            collective_id=0, has_side_effects=True, vmem_limit_bytes=15 * MIB
        ),
        name="gather_and_select",
    )(*(pltpu.with_memory_space_constraint(v, pltpu.HBM) for v in (x, g, w, mom[0])), sel)
    grad, res, new = pl.pallas_call(
        second_kernel,
        out_shape=(
            jax.ShapeDtypeStruct((1024, 2048), f32),
            jax.ShapeDtypeStruct((2048, 512), f32),
            jax.ShapeDtypeStruct((2048, 512), f32),
        ),
        in_specs=[vm] * 7,
        out_specs=[any_space] * 3,
        scratch_shapes=[
            pltpu.VMEM((4, 2048, 128), f32),
            pltpu.SemaphoreType.DMA((6,)),
        ],
        compiler_params=pltpu.CompilerParams(vmem_limit_bytes=12 * MIB),
        name="decode_and_write",
    )(*(pltpu.with_memory_space_constraint(v, pltpu.VMEM) for v in mid))
    return grad, res[None], new


def solution(mesh):
    in_specs = (P("rep", "feat"), P(("rep", "feat"), None), P("feat", None), P("rep", "feat", None), P())
    out_specs = (P("rep", "feat"), P("rep", "feat", None), P("feat", None))
    return jax.shard_map(body, mesh=mesh, in_specs=in_specs, out_specs=out_specs, check_vma=False)
```

time: 65.1 us -> 46.2 us (0.71)
  the two profiles are of different devices: /device:TPU:1 before, /device:TPU:0 now
where the time goes in v1:
time: 46.2 us; the launch traced here: 46 us
  Pallas kernels  44.5 us (96%)
  between operations  0.81 us (2%)
  local copies, waits for them, and re-layouts  0.71 us (2%)
    pallas_call x1, Pallas kernels, body(): pl.pallas_call(first_kernel, out_shape=(vmem((2048, 512), f32), vmem((102...  34.2 us
    pallas_call x1, Pallas kernels, body(): pl.pallas_call(second_kernel, out_shape=(jax.ShapeDtypeStruct((1024, 2048...  10.3 us

profile of v1, /device:TPU:0, one launch (start us, length us, event | category | flops | bytes accessed | tf_op | source)
XLA Modules:
  0.0 46.0 jit_solution(14873633439914197368)
XLA Ops:
  0.6 0.0 copy-start
  0.6 0.7 %copy-done = s32[32,32]{1,0:T(8,128)S(1)} copy-done((s32[32,32]{1,0:T(8,128)S(1)}, s32[32,32]{1,0:T(8,128)}, u32[]{:S(2)}) %copy-start) | copy-done | bytes 4120
  1.4 34.2 %gather_and_select.1 = (f32[2048,512]{1,0:T(8,128)S(1)}, f32[1024,2048]{1,0:T(8,128)S(1)}, bf16[4096,1024]{1,0:T(8,128)(2,1)S(1)}, bf16[4096,1024]{1,0:T(8,128)(...) custom-call(bf16[1024,2048]{1,0:T(8,128)(2,1)} %x_hbm.1, ...), custom_call_target="tpu_custom_call" | custom-call | tf_op jit(solution)/shard_map/gather_and_select/pallas_call | solution.py:296
  35.5 10.3 %decode_and_write.1 = (f32[1024,2048]{1,0:T(8,128)}, f32[2048,512]{1,0:T(8,128)}, f32[2048,512]{1,0:T(8,128)}) custom-call(f32[2048,512]{1,0:T(8,128)S(1)} %get-tuple-element.13.m_ref, f32[1024,2048]{1,0:T(8,128)S(1)} %get-tuple-element.14.grad_ref, bf16[4096,1024]{1,0:T(8,128)(2,1)S(1)} %get-tuple-element.15.eh_ref, ...), custom_call_target="tpu_custom_call" | custom-call | tf_op jit(solution)/shard_map/decode_and_write/pallas_call | solution.py:332
Async XLA Ops:
  0.6 0.7 %copy-start = (s32[32,32]{1,0:T(8,128)S(1)}, s32[32,32]{1,0:T(8,128)}, u32[]{:S(2)}) copy-start(s32[32,32]{1,0:T(8,128)} %sel_ref.1) | copy-start | bytes 12292

commit v2 on v1

v2 whole, which is shorter than its diff:
```python
import functools

import jax
import jax.numpy as jnp
from jax import lax
from jax.experimental import pallas as pl
from jax.experimental.pallas import tpu as pltpu
from jax.sharding import PartitionSpec as P

CH = 64
MOMENTUM_DECAY = 0.9
STEP_RATE = 0.5
f32 = jnp.float32
bf16 = jnp.bfloat16
NN = (((1,), (0,)), ((), ()))
NT = (((1,), (1,)), ((), ()))
TN = (((0,), (0,)), ((), ()))
MIB = 1 << 20


def dot(a, b, dims, precision=None):
    return lax.dot_general(a, b, dims, precision=precision, preferred_element_type=f32)


def split(v):
    high = v.astype(bf16)
    return high, (v - high.astype(f32)).astype(bf16)


def dct_transposed():
    a = lax.broadcasted_iota(jnp.int32, (CH, CH), 0)
    u = lax.broadcasted_iota(jnp.int32, (CH, CH), 1)
    turn = ((2 * a + 1) * u) & 255
    table = jnp.cos(turn.astype(f32) * f32(jnp.pi / 128)) * f32((2.0 / CH) ** 0.5)
    return jnp.where(u == 0, f32((1.0 / CH) ** 0.5), table)


def pick(table, row):
    n = row.shape[1]
    hot = (lax.broadcasted_iota(jnp.int32, (CH, n), 0) == jnp.broadcast_to(row, (CH, n))).astype(f32)
    return dot(table, hot, NN, lax.Precision.HIGHEST)


def offsets():
    both = [(dy, dz) for dy in range(4) for dz in range(4) if (dy, dz) != (0, 0)]
    return sorted(both, key=lambda o: (min(o[0], 4 - o[0]) + min(o[1], 4 - o[1]), o))


def first_kernel(
    x_hbm, g_hbm, w_hbm, mom_hbm, sel_hbm,
    m_ref, grad_ref, eh_ref, el_ref, sign_ref, own_ref, oth_ref, nw, wv, gv,
    xv, xt, sel_ref, but, bvt, bhl, bhh, bu4, cown, lh, ll,
    local_sem, g_send, g_recv, c_send, own_recv, oth_recv,
):
    feat = lax.axis_index("feat")
    rep = lax.axis_index("rep")
    core = rep % 2
    chip = rep // 2
    y, z = chip // 4, chip % 4
    partner = rep + 1 - 2 * core
    right, left, across = (feat + 1) % 4, (feat + 3) % 4, (feat + 2) % 4
    blocks = (feat, left, right, across)

    def chip_at(dy, dz):
        return (y + dy) % 4 * 4 + (z + dz) % 4

    barrier = pltpu.get_barrier_semaphore()
    for f in (left, right):
        pl.semaphore_signal(barrier, inc=1, device_id={"feat": f})
    for dy, dz in offsets():
        pl.semaphore_signal(barrier, inc=1, device_id={"rep": chip_at(dy, dz) * 2 + core})
    pl.semaphore_signal(barrier, inc=1, device_id={"rep": partner})

    sel_copy = pltpu.make_async_copy(sel_hbm, sel_ref, local_sem.at[0])
    own_g = [
        pltpu.make_async_copy(g_hbm.at[:, pl.ds(h * 256, 256)], gv.at[h, pl.ds(0, 256)], local_sem.at[1 + h])
        for h in range(2)
    ]
    x_copies = [
        pltpu.make_async_copy(x_hbm.at[pl.ds(b * 256, 256)], xv.at[pl.ds(n * 256, 256)], local_sem.at[3 + n])
        for n, b in enumerate(blocks)
    ]
    m_copy = pltpu.make_async_copy(mom_hbm, m_ref, local_sem.at[7])
    w_copies = [
        pltpu.make_async_copy(w_hbm.at[:, pl.ds(n * 128, 128)], wv.at[n], local_sem.at[8 + n]) for n in range(4)
    ]
    for cp in [sel_copy] + x_copies + own_g + [m_copy] + w_copies:
        cp.start()

    def g_copy(h, n, slot, half, to, forward=None):
        if forward is None:
            src = g_hbm.at[pl.ds(half * 128, 128), pl.ds(h * 256, 256)]
        else:
            src = gv.at[h, pl.ds(forward * 256 + half * 128, 128)]
        return pltpu.make_async_remote_copy(
            src_ref=src,
            dst_ref=gv.at[h, pl.ds(slot * 256 + half * 128, 128)],
            send_sem=g_send.at[h * 6 + n],
            recv_sem=g_recv.at[h * 6 + n],
            device_id={"feat": to},
        )

    sends = [
        [
            g_copy(h, 0, 1, 0, right),
            g_copy(h, 1, 2, 1, left),
            g_copy(h, 2, 1, 1, right),
            g_copy(h, 3, 2, 0, left),
            g_copy(h, 4, 3, 0, right, 1),
            g_copy(h, 5, 3, 1, left, 2),
        ]
        for h in range(2)
    ]
    pl.semaphore_wait(barrier, 18)
    for cp in sends[0][:4] + sends[1][:2]:
        cp.start()

    def forward(h):
        for n in range(2):
            sends[h][n].wait_recv()
            sends[h][4 + n].start()

    table = dct_transposed()
    sel_copy.wait()
    rows = []
    for s in range(32):
        plane = core if s < 16 else 1 - core
        rows.append(sel_ref[pl.ds((s % 16) * 2 + plane, 1), :])
    flat = jnp.concatenate(rows, axis=1)
    but[...] = pick(table, flat >> 6)
    bvt[...] = pick(table, flat & 63)
    sign_ref[...] = jnp.broadcast_to(f32(1) - f32(2) * ((flat >> 6) & 1).astype(f32), (8, 1024))
    mine = sel_ref[pl.ds(rep, 1), :]
    mine = jnp.concatenate([mine] * 4, axis=1)
    bu4[...] = pick(table, mine >> 6)
    tall = jnp.concatenate([pick(table, mine & 63)] * 4, axis=0)
    ahead = lax.broadcasted_iota(jnp.int32, (256, 128), 0) // 64
    along = lax.broadcasted_iota(jnp.int32, (256, 128), 1) // 32
    high, low = split(jnp.where(ahead == along, tall, f32(0)))
    bhl[:, :128] = high
    bhl[:, 128:] = low
    bhh[:, :128] = high
    bhh[:, 128:] = high

    for slot in range(4):
        x_copies[slot].wait()

        @pl.loop(0, 8)
        def _(n):
            a = slot * 8 + n
            high, low = split(but[pl.ds(a, 1), :] * bvt[...])
            to = pl.ds(pl.multiple_of(a * CH, CH), CH)
            eh_ref[to, :] = high
            el_ref[to, :] = low
            at = pl.ds(pl.multiple_of(n * 256, 256), 256)
            xt[slot, at, :] = xv[slot * 256 : slot * 256 + 256, at].T

        if slot == 2:
            forward(0)
            for cp in sends[1][2:4]:
                cp.start()

    gone = []

    def send(h, dst, sem, at, to):
        cp = pltpu.make_async_remote_copy(
            src_ref=own_ref.at[h, at],
            dst_ref=dst.at[h, at],
            send_sem=c_send.at[len(gone)],
            recv_sem=sem.at[h * 16 + at],
            device_id={"rep": to},
        )
        cp.start()
        gone.append(cp)

    def arrived(h, ref, sem, at):
        pltpu.make_async_remote_copy(
            src_ref=ref.at[h, at], dst_ref=ref.at[h, at], send_sem=c_send.at[0], recv_sem=sem.at[h * 16 + at],
            device_id={"rep": partner},
        ).wait_recv()

    def pass_on(h, n0, n1):
        for dy, dz in offsets()[n0:n1]:
            at = chip_at(-dy, -dz)
            arrived(h, own_ref, own_recv, at)
            send(h, oth_ref, oth_recv, at, partner)

    def momentum(h):
        own_g[h].wait()
        sends[h][2].wait_recv()
        sends[h][3].wait_recv()
        if h == 0:
            m_copy.wait()
        cols = slice(h * 256, h * 256 + 256)
        for n in range(4):
            at = slice(n * 512, n * 512 + 512)
            lhs = jnp.concatenate([xt[s, at, :] for s in range(3)], axis=1)
            part = dot(lhs, gv[h, 0:768, :], NN) * f32(1.0 / 1024)
            m_ref[at, cols] = f32(MOMENTUM_DECAY) * m_ref[at, cols] + part

    def coefficients(h):
        sends[h][4].wait_recv()
        sends[h][5].wait_recv()
        cols = slice(h * 256, h * 256 + 256)
        for n in range(4):
            at = slice(n * 512, n * 512 + 512)
            value = m_ref[at, cols] + dot(xt[3, at, :], gv[h, 768:1024, :], NN) * f32(1.0 / 1024)
            m_ref[at, cols] = value
            high, low = split(value)
            wide = dot(high, bhl[...], NN)
            inner = wide[:, :128] + wide[:, 128:] + dot(low, bhl[:, :128], NN)
            cown[h, n * 8 : n * 8 + 8, :] = jnp.sum(inner.reshape(8, CH, 128) * bu4[...][None], axis=1)
        turned = cown[h].T
        own_ref[h, chip] = jnp.concatenate([turned[j * 32 : j * 32 + 32, :] for j in range(4)], axis=1)
        for dy, dz in offsets():
            send(h, own_ref, own_recv, chip, chip_at(dy, dz) * 2 + core)
        send(h, oth_ref, oth_recv, chip, partner)

    momentum(0)
    forward(1)
    coefficients(0)
    momentum(1)
    coefficients(1)

    def take_away(h):
        for n in range(4):
            at, cols = slice(n * 512, n * 512 + 512), slice(h * 256, h * 256 + 256)
            field = cown[h, n * 8 : n * 8 + 8, :][:, None, :] * bu4[...][None]
            high, low = split(field.reshape(512, 128))
            back = dot(jnp.concatenate([high, low], axis=1), bhh[...], NT) + dot(high, bhl[:, 128:], NT)
            m_ref[at, cols] = m_ref[at, cols] - back

    for cp in w_copies:
        cp.wait()
    take_away(0)
    pass_on(0, 0, 8)
    rows = [pl.ds(pl.multiple_of(b * 256, 256), 256) for b in blocks]
    input_grad(0, wv, gv, grad_ref, rows, 0)
    pass_on(0, 8, 15)
    take_away(1)
    pass_on(1, 0, 8)
    input_grad(1, wv, gv, grad_ref, rows, 1)
    pass_on(1, 8, 15)
    for n in range(16):
        arrived(0, oth_ref, oth_recv, n)
    fill(0, own_ref, oth_ref, sign_ref, lh, ll)
    for n in range(4):
        decode(0, n, eh_ref, el_ref, lh, ll, wv, nw)
    for n in range(16):
        arrived(1, oth_ref, oth_recv, n)
    for cp in sends[0] + sends[1] + gone:
        cp.wait_send()


def input_grad(n, wv, gv, to, rows, place):
    at = slice(n * 512, n * 512 + 512)
    part = None
    for h in range(2):
        high, low = split(jnp.concatenate([wv[2 * h, at, :], wv[2 * h + 1, at, :]], axis=1))
        new = dot(gv[h], high, NT) + dot(gv[h], low, NT)
        part = new if part is None else part + new
    for s in range(4):
        to[rows[s], place * 512 : place * 512 + 512] = part[s * 256 : s * 256 + 256, :]


def fill(h, own_ref, oth_ref, sign_ref, lh, ll):
    both = jnp.concatenate([own_ref[h].reshape(512, 128), oth_ref[h].reshape(512, 128)], axis=0)
    turned = both.T * f32(STEP_RATE)
    mirrored = turned * sign_ref[0:1, :]
    high, low = split(jnp.concatenate([turned, mirrored], axis=0))
    lh[...] = high
    ll[...] = low


def decode(h, n, eh_ref, el_ref, lh, ll, w_ref, nw):
    low_half = lax.broadcasted_iota(jnp.int32, (32, 128), 1) < 64
    at = slice(n * 512, n * 512 + 512)
    eh = eh_ref[at, :]
    total = dot(lh[...], eh, NT) + dot(ll[...], eh, NT) + dot(lh[...], el_ref[at, :], NT)
    for side in range(2):
        for k in range(4):
            for j in range(2):
                top = side * 128 + j * 64
                one = total[top : top + 32, k * 128 : k * 128 + 128]
                two = total[top + 32 : top + 64, k * 128 : k * 128 + 128]
                even = jnp.where(low_half, one, pltpu.roll(two, 64, 1))
                odd = jnp.where(low_half, pltpu.roll(one, 64, 1), two)
                for o, v in enumerate((even, odd)):
                    a = n * 8 + k * 2 + o
                    rows = pl.ds(63 - a if side else a, 32, stride=CH)
                    nw[j, rows, :] = w_ref[2 * h + j, rows, :] - v


def second_kernel(
    m_ref, grad_ref, eh_ref, el_ref, sign_ref, own_ref, oth_ref, new_ref, w_ref, gv,
    grad_hbm, res_hbm, new_hbm, rest, nw, lh, ll, sems,
):
    feat = lax.axis_index("feat")
    blocks = (feat, (feat + 3) % 4, (feat + 1) % 4, (feat + 2) % 4)
    rows = [pl.ds(pl.multiple_of(b * 256, 256), 256) for b in blocks]
    copies = []

    def start(src, dst):
        cp = pltpu.make_async_copy(src, dst, sems.at[len(copies)])
        cp.start()
        copies.append(cp)

    start(grad_ref, grad_hbm.at[:, pl.ds(0, 1024)])
    start(m_ref, res_hbm)
    for j in range(2):
        start(new_ref.at[j], new_hbm.at[:, pl.ds(j * 128, 128)])
    for n in range(2):
        input_grad(2 + n, w_ref, gv, rest, rows, n)
        start(rest.at[:, pl.ds(n * 512, 512)], grad_hbm.at[:, pl.ds(1024 + n * 512, 512)])
    fill(1, own_ref, oth_ref, sign_ref, lh, ll)
    for n in range(4):
        decode(1, n, eh_ref, el_ref, lh, ll, w_ref, nw)
    for j in range(2):
        start(nw.at[j], new_hbm.at[:, pl.ds(256 + j * 128, 128)])
    for cp in copies:
        cp.wait()


def vmem(shape, dtype):
    return pltpu.VMEM(shape, dtype)


def body(x, g, w, mom, sel):
    any_space = pl.BlockSpec(memory_space=pl.ANY)
    vm = pl.BlockSpec(memory_space=pltpu.VMEM)
    mid = pl.pallas_call(
        first_kernel,
        out_shape=(
            vmem((2048, 512), f32),
            vmem((1024, 1024), f32),
            vmem((2048, 1024), bf16),
            vmem((2048, 1024), bf16),
            vmem((8, 1024), f32),
            vmem((2, 16, 32, 128), f32),
            vmem((2, 16, 32, 128), f32),
            vmem((2, 2048, 128), f32),
            vmem((4, 2048, 128), f32),
            vmem((2, 1024, 256), bf16),
        ),
        in_specs=[any_space] * 5,
        out_specs=[vm] * 10,
        scratch_shapes=[
            pltpu.VMEM((1024, 2048), bf16),
            pltpu.VMEM((4, 2048, 256), bf16),
            pltpu.VMEM((32, 32), jnp.int32),
            pltpu.VMEM((CH, 1024), f32),
            pltpu.VMEM((CH, 1024), f32),
            pltpu.VMEM((256, 256), bf16),
            pltpu.VMEM((256, 256), bf16),
            pltpu.VMEM((CH, 128), f32),
            pltpu.VMEM((2, 32, 128), f32),
            pltpu.VMEM((256, 1024), bf16),
            pltpu.VMEM((256, 1024), bf16),
            pltpu.SemaphoreType.DMA((12,)),
            pltpu.SemaphoreType.DMA((12,)),
            pltpu.SemaphoreType.DMA((12,)),
            pltpu.SemaphoreType.DMA((62,)),
            pltpu.SemaphoreType.DMA((32,)),
            pltpu.SemaphoreType.DMA((32,)),
        ],
        compiler_params=pltpu.CompilerParams(
            collective_id=0, has_side_effects=True, vmem_limit_bytes=18 * MIB
        ),
        name="gather_and_select",
    )(*(pltpu.with_memory_space_constraint(v, pltpu.HBM) for v in (x, g, w, mom[0], sel)))
    grad, res, new = pl.pallas_call(
        second_kernel,
        out_shape=(
            jax.ShapeDtypeStruct((1024, 2048), f32),
            jax.ShapeDtypeStruct((2048, 512), f32),
            jax.ShapeDtypeStruct((2048, 512), f32),
        ),
        in_specs=[vm] * 10,
        out_specs=[any_space] * 3,
        scratch_shapes=[
            pltpu.VMEM((1024, 1024), f32),
            pltpu.VMEM((2, 2048, 128), f32),
            pltpu.VMEM((256, 1024), bf16),
            pltpu.VMEM((256, 1024), bf16),
            pltpu.SemaphoreType.DMA((16,)),
        ],
        compiler_params=pltpu.CompilerParams(vmem_limit_bytes=14 * MIB),
        name="decode_and_write",
    )(*(pltpu.with_memory_space_constraint(v, pltpu.VMEM) for v in mid))
    return grad, res[None], new


def solution(mesh):
    in_specs = (P("rep", "feat"), P(("rep", "feat"), None), P("feat", None), P("rep", "feat", None), P())
    out_specs = (P("rep", "feat"), P("rep", "feat", None), P("feat", None))
    return jax.shard_map(body, mesh=mesh, in_specs=in_specs, out_specs=out_specs, check_vma=False)
```

time: 46.2 us -> 44 us (0.952)
  the two profiles are of different devices: /device:TPU:0 before, /device:TPU:1 now
where the time goes in v2:
time: 44 us; the launch traced here: 43.4 us
  Pallas kernels  42.6 us (97%)
  between operations  0.8 us (2%)
    pallas_call x1, Pallas kernels, body(): pl.pallas_call(first_kernel, out_shape=(vmem((2048, 512), f32), vmem((102...  33.3 us
    pallas_call x1, Pallas kernels, body(): pl.pallas_call(second_kernel, out_shape=(jax.ShapeDtypeStruct((1024, 2048...  9.26 us

profile of v2, /device:TPU:1, one launch (start us, length us, event | category | flops | bytes accessed | tf_op | source)
XLA Modules:
  0.0 43.4 jit_solution(12288614850533352445)
XLA Ops:
  0.6 33.3 %gather_and_select.1 = (f32[2048,512]{1,0:T(8,128)S(1)}, f32[1024,1024]{1,0:T(8,128)S(1)}, bf16[2048,1024]{1,0:T(8,128)(2,1)S(1)}, bf16[2048,1024]{1,0:T(8,128)(...) custom-call(bf16[1024,2048]{1,0:T(8,128)(2,1)} %x_hbm.1, ...), custom_call_target="tpu_custom_call" | custom-call | tf_op jit(solution)/shard_map/gather_and_select/pallas_call | solution.py:331
  34.0 9.3 %decode_and_write.1 = (f32[1024,2048]{1,0:T(8,128)}, f32[2048,512]{1,0:T(8,128)}, f32[2048,512]{1,0:T(8,128)}) custom-call(f32[2048,512]{1,0:T(8,128)S(1)} %get-tuple-element.16.m_ref, f32[1024,1024]{1,0:T(8,128)S(1)} %get-tuple-element.17.grad_ref, bf16[2048,1024]{1,0:T(8,128)(2,1)S(1)} %get-tuple-element.18.eh_ref, ...), custom_call_target="tpu_custom_call" | custom-call | tf_op jit(solution)/shard_map/decode_and_write/pallas_call | solution.py:371

commit v3 on v2

--- a/solution.py
+++ b/solution.py
@@ -82,9 +82,9 @@
     ]
     m_copy = pltpu.make_async_copy(mom_hbm, m_ref, local_sem.at[7])
     w_copies = [
-        pltpu.make_async_copy(w_hbm.at[:, pl.ds(n * 128, 128)], wv.at[n], local_sem.at[8 + n]) for n in range(4)
+        pltpu.make_async_copy(w_hbm.at[:, :, pl.ds(n * 128, 128)], wv.at[n], local_sem.at[8 + n]) for n in range(4)
     ]
-    for cp in [sel_copy] + x_copies + own_g + [m_copy] + w_copies:
+    for cp in [sel_copy] + x_copies:
         cp.start()
 
     def g_copy(h, n, slot, half, to, forward=None):
@@ -122,6 +122,8 @@
 
     table = dct_transposed()
     sel_copy.wait()
+    for cp in own_g + [m_copy]:
+        cp.start()
     rows = []
     for s in range(32):
         plane = core if s < 16 else 1 - core
@@ -155,9 +157,9 @@
             at = pl.ds(pl.multiple_of(n * 256, 256), 256)
             xt[slot, at, :] = xv[slot * 256 : slot * 256 + 256, at].T
 
-        if slot == 2:
+        if slot == 1:
             forward(0)
-            for cp in sends[1][2:4]:
+            for cp in sends[1][2:4] + w_copies:
                 cp.start()
 
     gone = []
@@ -212,12 +214,12 @@
             cown[h, n * 8 : n * 8 + 8, :] = jnp.sum(inner.reshape(8, CH, 128) * bu4[...][None], axis=1)
         turned = cown[h].T
         own_ref[h, chip] = jnp.concatenate([turned[j * 32 : j * 32 + 32, :] for j in range(4)], axis=1)
-        for dy, dz in offsets():
+        for dy, dz in offsets()[::-1]:
             send(h, own_ref, own_recv, chip, chip_at(dy, dz) * 2 + core)
         send(h, oth_ref, oth_recv, chip, partner)
 
+    forward(1)
     momentum(0)
-    forward(1)
     coefficients(0)
     momentum(1)
     coefficients(1)
@@ -230,21 +232,23 @@
             back = dot(jnp.concatenate([high, low], axis=1), bhh[...], NT) + dot(high, bhl[:, 128:], NT)
             m_ref[at, cols] = m_ref[at, cols] - back
 
+    rows = [pl.ds(pl.multiple_of(b * 256, 256), 256) for b in blocks]
+    pass_on(0, 0, 8)
+    take_away(0)
+    take_away(1)
+    pass_on(0, 8, 15)
     for cp in w_copies:
         cp.wait()
-    take_away(0)
-    pass_on(0, 0, 8)
-    rows = [pl.ds(pl.multiple_of(b * 256, 256), 256) for b in blocks]
     input_grad(0, wv, gv, grad_ref, rows, 0)
-    pass_on(0, 8, 15)
-    take_away(1)
-    pass_on(1, 0, 8)
+    pass_on(1, 0, 4)
     input_grad(1, wv, gv, grad_ref, rows, 1)
-    pass_on(1, 8, 15)
+    pass_on(1, 4, 10)
     for n in range(16):
         arrived(0, oth_ref, oth_recv, n)
     fill(0, own_ref, oth_ref, sign_ref, lh, ll)
-    for n in range(4):
+    decode(0, 0, eh_ref, el_ref, lh, ll, wv, nw)
+    pass_on(1, 10, 15)
+    for n in range(1, 4):
         decode(0, n, eh_ref, el_ref, lh, ll, wv, nw)
     for n in range(16):
         arrived(1, oth_ref, oth_recv, n)
@@ -253,10 +257,10 @@
 
 
 def input_grad(n, wv, gv, to, rows, place):
-    at = slice(n * 512, n * 512 + 512)
     part = None
     for h in range(2):
-        high, low = split(jnp.concatenate([wv[2 * h, at, :], wv[2 * h + 1, at, :]], axis=1))
+        pair = [wv[2 * h + k, n * 8 : n * 8 + 8].reshape(512, 128) for k in range(2)]
+        high, low = split(jnp.concatenate(pair, axis=1))
         new = dot(gv[h], high, NT) + dot(gv[h], low, NT)
         part = new if part is None else part + new
     for s in range(4):
@@ -278,17 +282,19 @@
     eh = eh_ref[at, :]
     total = dot(lh[...], eh, NT) + dot(ll[...], eh, NT) + dot(lh[...], el_ref[at, :], NT)
     for side in range(2):
-        for k in range(4):
-            for j in range(2):
+        for j in range(2):
+            vals = []
+            for k in range(4):
                 top = side * 128 + j * 64
                 one = total[top : top + 32, k * 128 : k * 128 + 128]
                 two = total[top + 32 : top + 64, k * 128 : k * 128 + 128]
-                even = jnp.where(low_half, one, pltpu.roll(two, 64, 1))
-                odd = jnp.where(low_half, pltpu.roll(one, 64, 1), two)
-                for o, v in enumerate((even, odd)):
-                    a = n * 8 + k * 2 + o
-                    rows = pl.ds(63 - a if side else a, 32, stride=CH)
-                    nw[j, rows, :] = w_ref[2 * h + j, rows, :] - v
+                vals.append(jnp.where(low_half, one, pltpu.roll(two, 64, 1)))
+                vals.append(jnp.where(low_half, pltpu.roll(one, 64, 1), two))
+            first = 56 - 8 * n if side else 8 * n
+            if side:
+                vals = vals[::-1]
+            rows = slice(first, first + 8)
+            nw[j, :, rows, :] = w_ref[2 * h + j, :, rows, :] - jnp.swapaxes(jnp.stack(vals, axis=0), 0, 1)
 
 
 def second_kernel(
@@ -308,15 +314,17 @@
     start(grad_ref, grad_hbm.at[:, pl.ds(0, 1024)])
     start(m_ref, res_hbm)
     for j in range(2):
-        start(new_ref.at[j], new_hbm.at[:, pl.ds(j * 128, 128)])
+        start(new_ref.at[j], new_hbm.at[:, :, pl.ds(j * 128, 128)])
     for n in range(2):
         input_grad(2 + n, w_ref, gv, rest, rows, n)
         start(rest.at[:, pl.ds(n * 512, 512)], grad_hbm.at[:, pl.ds(1024 + n * 512, 512)])
     fill(1, own_ref, oth_ref, sign_ref, lh, ll)
     for n in range(4):
         decode(1, n, eh_ref, el_ref, lh, ll, w_ref, nw)
-    for j in range(2):
-        start(nw.at[j], new_hbm.at[:, pl.ds(256 + j * 128, 128)])
+        for first in (8 * n, 56 - 8 * n):
+            for j in range(2):
+                part = pl.ds(first, 8)
+                start(nw.at[j, :, part], new_hbm.at[:, part, pl.ds(256 + j * 128, 128)])
     for cp in copies:
         cp.wait()
 
@@ -338,8 +346,8 @@
             vmem((8, 1024), f32),
             vmem((2, 16, 32, 128), f32),
             vmem((2, 16, 32, 128), f32),
-            vmem((2, 2048, 128), f32),
-            vmem((4, 2048, 128), f32),
+            vmem((2, 32, CH, 128), f32),
+            vmem((4, 32, CH, 128), f32),
             vmem((2, 1024, 256), bf16),
         ),
         in_specs=[any_space] * 5,
@@ -367,27 +375,27 @@
             collective_id=0, has_side_effects=True, vmem_limit_bytes=18 * MIB
         ),
         name="gather_and_select",
-    )(*(pltpu.with_memory_space_constraint(v, pltpu.HBM) for v in (x, g, w, mom[0], sel)))
+    )(*(pltpu.with_memory_space_constraint(v, pltpu.HBM) for v in (x, g, w.reshape(32, CH, 512), mom[0], sel)))
     grad, res, new = pl.pallas_call(
         second_kernel,
         out_shape=(
             jax.ShapeDtypeStruct((1024, 2048), f32),
             jax.ShapeDtypeStruct((2048, 512), f32),
-            jax.ShapeDtypeStruct((2048, 512), f32),
+            jax.ShapeDtypeStruct((32, CH, 512), f32),
         ),
         in_specs=[vm] * 10,
         out_specs=[any_space] * 3,
         scratch_shapes=[
             pltpu.VMEM((1024, 1024), f32),
-            pltpu.VMEM((2, 2048, 128), f32),
+            pltpu.VMEM((2, 32, CH, 128), f32),
             pltpu.VMEM((256, 1024), bf16),
             pltpu.VMEM((256, 1024), bf16),
-            pltpu.SemaphoreType.DMA((16,)),
+            pltpu.SemaphoreType.DMA((22,)),
         ],
         compiler_params=pltpu.CompilerParams(vmem_limit_bytes=14 * MIB),
         name="decode_and_write",
     )(*(pltpu.with_memory_space_constraint(v, pltpu.VMEM) for v in mid))
-    return grad, res[None], new
+    return grad, res[None], new.reshape(2048, 512)
 
 
 def solution(mesh):

time: 44 us -> 42.1 us (0.957)
  Pallas kernels: 42.6 us -> 40.7 us
    pallas_call x1, Pallas kernels: 9.26 us -> 7.18 us  [body(): pl.pallas_call(second_kernel, out_shape=(jax.ShapeDtypeStruct((1024, 2048...]
where the time goes in v3:
time: 42.1 us; the launch traced here: 41.5 us
  Pallas kernels  40.7 us (97%)
  between operations  0.8 us (2%)
    pallas_call x1, Pallas kernels, body(): pl.pallas_call(first_kernel, out_shape=(vmem((2048, 512), f32), vmem((102...  33.5 us
    pallas_call x1, Pallas kernels, body(): pl.pallas_call(second_kernel, out_shape=(jax.ShapeDtypeStruct((1024, 2048...  7.18 us

profile of v3, /device:TPU:1, one launch (start us, length us, event | category | flops | bytes accessed | tf_op | source)
XLA Modules:
  0.0 41.5 jit_solution(15955185648933326088)
XLA Ops:
  0.6 33.5 %gather_and_select.1 = (f32[2048,512]{1,0:T(8,128)S(1)}, f32[1024,1024]{1,0:T(8,128)S(1)}, bf16[2048,1024]{1,0:T(8,128)(2,1)S(1)}, bf16[2048,1024]{1,0:T(8,128)(...) custom-call(bf16[1024,2048]{1,0:T(8,128)(2,1)} %x_hbm.1, ...), custom_call_target="tpu_custom_call" | custom-call | tf_op jit(solution)/shard_map/gather_and_select/pallas_call | solution.py:339
  34.2 7.2 %decode_and_write.1 = (f32[1024,2048]{1,0:T(8,128)}, f32[2048,512]{1,0:T(8,128)}, f32[32,64,512]{2,1,0:T(8,128)}) custom-call(f32[2048,512]{1,0:T(8,128)S(1)} %get-tuple-element.16.m_ref, f32[1024,1024]{1,0:T(8,128)S(1)} %get-tuple-element.17.grad_ref, bf16[2048,1024]{1,0:T(8,128)(2,1)S(1)} %get-tuple-element.18.eh_ref, ...), custom_call_target="tpu_custom_call" | custom-call | tf_op jit(solution)/shard_map/decode_and_write/pallas_call | solution.py:379

commit v4 on v3

--- a/solution.py
+++ b/solution.py
@@ -49,7 +49,7 @@
 def first_kernel(
     x_hbm, g_hbm, w_hbm, mom_hbm, sel_hbm,
     m_ref, grad_ref, eh_ref, el_ref, sign_ref, own_ref, oth_ref, nw, wv, gv,
-    xv, xt, sel_ref, but, bvt, bhl, bhh, bu4, cown, lh, ll,
+    xv, xt, sel_ref, but, bvt, bhl, bhh, bu4, cown, lh, ll, acc,
     local_sem, g_send, g_recv, c_send, own_recv, oth_recv,
 ):
     feat = lax.axis_index("feat")
@@ -69,6 +69,7 @@
         pl.semaphore_signal(barrier, inc=1, device_id={"feat": f})
     for dy, dz in offsets():
         pl.semaphore_signal(barrier, inc=1, device_id={"rep": chip_at(dy, dz) * 2 + core})
+        pl.semaphore_signal(barrier, inc=1, device_id={"rep": chip_at(dy, dz) * 2 + 1 - core})
     pl.semaphore_signal(barrier, inc=1, device_id={"rep": partner})
 
     sel_copy = pltpu.make_async_copy(sel_hbm, sel_ref, local_sem.at[0])
@@ -111,7 +112,7 @@
         ]
         for h in range(2)
     ]
-    pl.semaphore_wait(barrier, 18)
+    pl.semaphore_wait(barrier, 33)
     for cp in sends[0][:4] + sends[1][:2]:
         cp.start()
 
@@ -149,18 +150,21 @@
 
         @pl.loop(0, 8)
         def _(n):
-            a = slot * 8 + n
+            at = pl.ds(pl.multiple_of(n * 256, 256), 256)
+            xt[slot, at, :] = xv[slot * 256 : slot * 256 + 256, at].T
+
+        if slot == 3:
+            forward(0)
+            for cp in sends[1][2:4] + w_copies:
+                cp.start()
+
+    def outer(first, last):
+        @pl.loop(first, last)
+        def _(a):
             high, low = split(but[pl.ds(a, 1), :] * bvt[...])
             to = pl.ds(pl.multiple_of(a * CH, CH), CH)
             eh_ref[to, :] = high
             el_ref[to, :] = low
-            at = pl.ds(pl.multiple_of(n * 256, 256), 256)
-            xt[slot, at, :] = xv[slot * 256 : slot * 256 + 256, at].T
-
-        if slot == 1:
-            forward(0)
-            for cp in sends[1][2:4] + w_copies:
-                cp.start()
 
     gone = []
 
@@ -216,10 +220,14 @@
         own_ref[h, chip] = jnp.concatenate([turned[j * 32 : j * 32 + 32, :] for j in range(4)], axis=1)
         for dy, dz in offsets()[::-1]:
             send(h, own_ref, own_recv, chip, chip_at(dy, dz) * 2 + core)
+            if h == 1:
+                send(h, oth_ref, oth_recv, chip, chip_at(dy, dz) * 2 + 1 - core)
         send(h, oth_ref, oth_recv, chip, partner)
 
+    outer(0, 8)
+    momentum(0)
     forward(1)
-    momentum(0)
+    outer(8, 32)
     coefficients(0)
     momentum(1)
     coefficients(1)
@@ -233,23 +241,27 @@
             m_ref[at, cols] = m_ref[at, cols] - back
 
     rows = [pl.ds(pl.multiple_of(b * 256, 256), 256) for b in blocks]
-    pass_on(0, 0, 8)
     take_away(0)
     take_away(1)
-    pass_on(0, 8, 15)
+    pass_on(0, 0, 8)
     for cp in w_copies:
         cp.wait()
     input_grad(0, wv, gv, grad_ref, rows, 0)
-    pass_on(1, 0, 4)
+    pass_on(0, 8, 15)
+    fill(own_ref, 0, 0, sign_ref, lh, ll)
+    acc[:, 0:512] = product(0, 0, 512, eh_ref, el_ref, lh, ll)
+    acc[:, 512:1024] = product(1, 0, 512, eh_ref, el_ref, lh, ll)
+    acc[:, 1024:1536] = product(2, 0, 512, eh_ref, el_ref, lh, ll)
+    acc[:, 1536:2048] = product(3, 0, 512, eh_ref, el_ref, lh, ll)
     input_grad(1, wv, gv, grad_ref, rows, 1)
-    pass_on(1, 4, 10)
     for n in range(16):
         arrived(0, oth_ref, oth_recv, n)
-    fill(0, own_ref, oth_ref, sign_ref, lh, ll)
-    decode(0, 0, eh_ref, el_ref, lh, ll, wv, nw)
-    pass_on(1, 10, 15)
-    for n in range(1, 4):
-        decode(0, n, eh_ref, el_ref, lh, ll, wv, nw)
+    fill(oth_ref, 0, 1, sign_ref, lh, ll)
+    for n in range(4):
+        total = acc[:, n * 512 : n * 512 + 512] + product(n, 512, 1024, eh_ref, el_ref, lh, ll)
+        place(0, n, total, wv, nw)
+    for dy, dz in offsets():
+        arrived(1, own_ref, own_recv, chip_at(-dy, -dz))
     for n in range(16):
         arrived(1, oth_ref, oth_recv, n)
     for cp in sends[0] + sends[1] + gone:
@@ -267,20 +279,22 @@
         to[rows[s], place * 512 : place * 512 + 512] = part[s * 256 : s * 256 + 256, :]
 
 
-def fill(h, own_ref, oth_ref, sign_ref, lh, ll):
-    both = jnp.concatenate([own_ref[h].reshape(512, 128), oth_ref[h].reshape(512, 128)], axis=0)
-    turned = both.T * f32(STEP_RATE)
-    mirrored = turned * sign_ref[0:1, :]
-    high, low = split(jnp.concatenate([turned, mirrored], axis=0))
-    lh[...] = high
-    ll[...] = low
-
-
-def decode(h, n, eh_ref, el_ref, lh, ll, w_ref, nw):
+def fill(ref, h, half, sign_ref, lh, ll):
+    at = slice(half * 512, half * 512 + 512)
+    turned = ref[h].reshape(512, 128).T * f32(STEP_RATE)
+    high, low = split(jnp.concatenate([turned, turned * sign_ref[0:1, at]], axis=0))
+    lh[:, at] = high
+    ll[:, at] = low
+
+
+def product(n, first, last, eh_ref, el_ref, lh, ll):
+    at, terms = slice(n * 512, n * 512 + 512), slice(first, last)
+    high, low, eh = lh[:, terms], ll[:, terms], eh_ref[at, terms]
+    return dot(high, eh, NT) + dot(low, eh, NT) + dot(high, el_ref[at, terms], NT)
+
+
+def place(h, n, total, w_ref, nw):
     low_half = lax.broadcasted_iota(jnp.int32, (32, 128), 1) < 64
-    at = slice(n * 512, n * 512 + 512)
-    eh = eh_ref[at, :]
-    total = dot(lh[...], eh, NT) + dot(ll[...], eh, NT) + dot(lh[...], el_ref[at, :], NT)
     for side in range(2):
         for j in range(2):
             vals = []
@@ -318,9 +332,10 @@
     for n in range(2):
         input_grad(2 + n, w_ref, gv, rest, rows, n)
         start(rest.at[:, pl.ds(n * 512, 512)], grad_hbm.at[:, pl.ds(1024 + n * 512, 512)])
-    fill(1, own_ref, oth_ref, sign_ref, lh, ll)
+    fill(own_ref, 1, 0, sign_ref, lh, ll)
+    fill(oth_ref, 1, 1, sign_ref, lh, ll)
     for n in range(4):
-        decode(1, n, eh_ref, el_ref, lh, ll, w_ref, nw)
+        place(1, n, product(n, 0, 1024, eh_ref, el_ref, lh, ll), w_ref, nw)
         for first in (8 * n, 56 - 8 * n):
             for j in range(2):
                 part = pl.ds(first, 8)
@@ -364,6 +379,7 @@
             pltpu.VMEM((2, 32, 128), f32),
             pltpu.VMEM((256, 1024), bf16),
             pltpu.VMEM((256, 1024), bf16),
+            pltpu.VMEM((256, 2048), f32),
             pltpu.SemaphoreType.DMA((12,)),
             pltpu.SemaphoreType.DMA((12,)),
             pltpu.SemaphoreType.DMA((12,)),

time: 42.1 us -> 39.2 us (0.931)
  Pallas kernels: 40.7 us -> 38.1 us
    pallas_call x1, Pallas kernels: 33.5 us -> 31.2 us  [body(): pl.pallas_call(first_kernel, out_shape=(vmem((2048, 512), f32), vmem((102...]
where the time goes in v4:
time: 39.2 us; the launch traced here: 38.8 us
  Pallas kernels  38.1 us (97%)
  between operations  0.64 us (2%)
    pallas_call x1, Pallas kernels, body(): pl.pallas_call(first_kernel, out_shape=(vmem((2048, 512), f32), vmem((102...  31.2 us
    pallas_call x1, Pallas kernels, body(): pl.pallas_call(second_kernel, out_shape=(jax.ShapeDtypeStruct((1024, 2048...  6.97 us

profile of v4, /device:TPU:1, one launch (start us, length us, event | category | flops | bytes accessed | tf_op | source)
XLA Modules:
  0.0 38.8 jit_solution(16387366353800988252)
XLA Ops:
  0.6 31.2 %gather_and_select.1 = (f32[2048,512]{1,0:T(8,128)S(1)}, f32[1024,1024]{1,0:T(8,128)S(1)}, bf16[2048,1024]{1,0:T(8,128)(2,1)S(1)}, bf16[2048,1024]{1,0:T(8,128)(...) custom-call(bf16[1024,2048]{1,0:T(8,128)(2,1)} %x_hbm.1, ...), custom_call_target="tpu_custom_call" | custom-call | tf_op jit(solution)/shard_map/gather_and_select/pallas_call | solution.py:354
  31.8 7.0 %decode_and_write.1 = (f32[1024,2048]{1,0:T(8,128)}, f32[2048,512]{1,0:T(8,128)}, f32[32,64,512]{2,1,0:T(8,128)}) custom-call(f32[2048,512]{1,0:T(8,128)S(1)} %get-tuple-element.16.m_ref, f32[1024,1024]{1,0:T(8,128)S(1)} %get-tuple-element.17.grad_ref, bf16[2048,1024]{1,0:T(8,128)(2,1)S(1)} %get-tuple-element.18.eh_ref, ...), custom_call_target="tpu_custom_call" | custom-call | tf_op jit(solution)/shard_map/decode_and_write/pallas_call | solution.py:395

commit v5 on v4

--- a/solution.py
+++ b/solution.py
@@ -243,11 +243,10 @@
     rows = [pl.ds(pl.multiple_of(b * 256, 256), 256) for b in blocks]
     take_away(0)
     take_away(1)
-    pass_on(0, 0, 8)
     for cp in w_copies:
         cp.wait()
     input_grad(0, wv, gv, grad_ref, rows, 0)
-    pass_on(0, 8, 15)
+    pass_on(0, 0, 15)
     fill(own_ref, 0, 0, sign_ref, lh, ll)
     acc[:, 0:512] = product(0, 0, 512, eh_ref, el_ref, lh, ll)
     acc[:, 512:1024] = product(1, 0, 512, eh_ref, el_ref, lh, ll)

time: 39.2 us -> 38.9 us (level)
  no operation moved by 1% of the time
where the time goes in v5:
time: 38.9 us; the launch traced here: 38.8 us
  Pallas kernels  38.1 us (98%)
  between operations  0.64 us (2%)
    pallas_call x1, Pallas kernels, body(): pl.pallas_call(first_kernel, out_shape=(vmem((2048, 512), f32), vmem((102...  31.2 us
    pallas_call x1, Pallas kernels, body(): pl.pallas_call(second_kernel, out_shape=(jax.ShapeDtypeStruct((1024, 2048...  6.97 us

profile of v5, /device:TPU:1, one launch (start us, length us, event | category | flops | bytes accessed | tf_op | source)
XLA Modules:
  0.0 38.8 jit_solution(6284715743961007966)
XLA Ops:
  0.6 31.2 %gather_and_select.1 = (f32[2048,512]{1,0:T(8,128)S(1)}, f32[1024,1024]{1,0:T(8,128)S(1)}, bf16[2048,1024]{1,0:T(8,128)(2,1)S(1)}, bf16[2048,1024]{1,0:T(8,128)(...) custom-call(bf16[1024,2048]{1,0:T(8,128)(2,1)} %x_hbm.1, ...), custom_call_target="tpu_custom_call" | custom-call | tf_op jit(solution)/shard_map/gather_and_select/pallas_call | solution.py:353
  31.8 7.0 %decode_and_write.1 = (f32[1024,2048]{1,0:T(8,128)}, f32[2048,512]{1,0:T(8,128)}, f32[32,64,512]{2,1,0:T(8,128)}) custom-call(f32[2048,512]{1,0:T(8,128)S(1)} %get-tuple-element.16.m_ref, f32[1024,1024]{1,0:T(8,128)S(1)} %get-tuple-element.17.grad_ref, bf16[2048,1024]{1,0:T(8,128)(2,1)S(1)} %get-tuple-element.18.eh_ref, ...), custom_call_target="tpu_custom_call" | custom-call | tf_op jit(solution)/shard_map/decode_and_write/pallas_call | solution.py:394

commit v6 on v5

--- a/solution.py
+++ b/solution.py
@@ -48,7 +48,7 @@
 
 def first_kernel(
     x_hbm, g_hbm, w_hbm, mom_hbm, sel_hbm,
-    m_ref, grad_ref, eh_ref, el_ref, sign_ref, own_ref, oth_ref, nw, wv, gv,
+    m_ref, grad_ref, eh_ref, el_ref, sign_ref, own_ref, oth_ref, nw, wv, gv, high_ref, low_ref,
     xv, xt, sel_ref, but, bvt, bhl, bhh, bu4, cown, lh, ll, acc,
     local_sem, g_send, g_recv, c_send, own_recv, oth_recv,
 ):
@@ -224,14 +224,6 @@
                 send(h, oth_ref, oth_recv, chip, chip_at(dy, dz) * 2 + 1 - core)
         send(h, oth_ref, oth_recv, chip, partner)
 
-    outer(0, 8)
-    momentum(0)
-    forward(1)
-    outer(8, 32)
-    coefficients(0)
-    momentum(1)
-    coefficients(1)
-
     def take_away(h):
         for n in range(4):
             at, cols = slice(n * 512, n * 512 + 512), slice(h * 256, h * 256 + 256)
@@ -240,8 +232,16 @@
             back = dot(jnp.concatenate([high, low], axis=1), bhh[...], NT) + dot(high, bhl[:, 128:], NT)
             m_ref[at, cols] = m_ref[at, cols] - back
 
+    outer(0, 8)
+    momentum(0)
+    forward(1)
+    outer(8, 32)
+    coefficients(0)
+    take_away(0)
+    momentum(1)
+    coefficients(1)
+
     rows = [pl.ds(pl.multiple_of(b * 256, 256), 256) for b in blocks]
-    take_away(0)
     take_away(1)
     for cp in w_copies:
         cp.wait()
@@ -261,6 +261,7 @@
         place(0, n, total, wv, nw)
     for dy, dz in offsets():
         arrived(1, own_ref, own_recv, chip_at(-dy, -dz))
+    fill(own_ref, 1, 0, sign_ref, high_ref, low_ref)
     for n in range(16):
         arrived(1, oth_ref, oth_recv, n)
     for cp in sends[0] + sends[1] + gone:
@@ -311,7 +312,7 @@
 
 
 def second_kernel(
-    m_ref, grad_ref, eh_ref, el_ref, sign_ref, own_ref, oth_ref, new_ref, w_ref, gv,
+    m_ref, grad_ref, eh_ref, el_ref, sign_ref, own_ref, oth_ref, new_ref, w_ref, gv, high_ref, low_ref,
     grad_hbm, res_hbm, new_hbm, rest, nw, lh, ll, sems,
 ):
     feat = lax.axis_index("feat")
@@ -331,7 +332,8 @@
     for n in range(2):
         input_grad(2 + n, w_ref, gv, rest, rows, n)
         start(rest.at[:, pl.ds(n * 512, 512)], grad_hbm.at[:, pl.ds(1024 + n * 512, 512)])
-    fill(own_ref, 1, 0, sign_ref, lh, ll)
+    lh[:, 0:512] = high_ref[...]
+    ll[:, 0:512] = low_ref[...]
     fill(oth_ref, 1, 1, sign_ref, lh, ll)
     for n in range(4):
         place(1, n, product(n, 0, 1024, eh_ref, el_ref, lh, ll), w_ref, nw)
@@ -363,9 +365,11 @@
             vmem((2, 32, CH, 128), f32),
             vmem((4, 32, CH, 128), f32),
             vmem((2, 1024, 256), bf16),
+            vmem((256, 512), bf16),
+            vmem((256, 512), bf16),
         ),
         in_specs=[any_space] * 5,
-        out_specs=[vm] * 10,
+        out_specs=[vm] * 12,
         scratch_shapes=[
             pltpu.VMEM((1024, 2048), bf16),
             pltpu.VMEM((4, 2048, 256), bf16),
@@ -398,7 +402,7 @@
             jax.ShapeDtypeStruct((2048, 512), f32),
             jax.ShapeDtypeStruct((32, CH, 512), f32),
         ),
-        in_specs=[vm] * 10,
+        in_specs=[vm] * 12,
         out_specs=[any_space] * 3,
         scratch_shapes=[
             pltpu.VMEM((1024, 1024), f32),

time: 38.9 us -> 38.9 us (level)
  no operation moved by 1% of the time
where the time goes in v6:
time: 38.9 us; the launch traced here: 38.8 us
  Pallas kernels  38.2 us (98%)
  between operations  0.64 us (2%)
    pallas_call x1, Pallas kernels, body(): pl.pallas_call(first_kernel, out_shape=(vmem((2048, 512), f32), vmem((102...  31.2 us
    pallas_call x1, Pallas kernels, body(): pl.pallas_call(second_kernel, out_shape=(jax.ShapeDtypeStruct((1024, 2048...  6.97 us

profile of v6, /device:TPU:1, one launch (start us, length us, event | category | flops | bytes accessed | tf_op | source)
XLA Modules:
  0.0 38.8 jit_solution(2932156551765046742)
XLA Ops:
  0.6 31.2 %gather_and_select.1 = (f32[2048,512]{1,0:T(8,128)S(1)}, f32[1024,1024]{1,0:T(8,128)S(1)}, bf16[2048,1024]{1,0:T(8,128)(2,1)S(1)}, bf16[2048,1024]{1,0:T(8,128)(...) custom-call(bf16[1024,2048]{1,0:T(8,128)(2,1)} %x_hbm.1, ...), custom_call_target="tpu_custom_call" | custom-call | tf_op jit(solution)/shard_map/gather_and_select/pallas_call | solution.py:355
  31.8 7.0 %decode_and_write.1 = (f32[1024,2048]{1,0:T(8,128)}, f32[2048,512]{1,0:T(8,128)}, f32[32,64,512]{2,1,0:T(8,128)}) custom-call(f32[2048,512]{1,0:T(8,128)S(1)} %get-tuple-element.18.m_ref, f32[1024,1024]{1,0:T(8,128)S(1)} %get-tuple-element.19.grad_ref, bf16[2048,1024]{1,0:T(8,128)(2,1)S(1)} %get-tuple-element.20.eh_ref, ...), custom_call_target="tpu_custom_call" | custom-call | tf_op jit(solution)/shard_map/decode_and_write/pallas_call | solution.py:398
